TPU v7x, 32 devices: a whole 2x2x4 slice. The times are simulated.
32 devices in a mesh: section: 2 (over y), dp: 4 (over x, core), mp: 4 (over z).
Axes of the slice: x: 2, y: 2, z: 4, core: 2. Of those that a mesh axis runs over, the one named last changes fastest.
Arguments:
- activations: bfloat16 [2, 256, 4096], P(None, 'dp'), may hold values from -6 to 6
- cotangent: bfloat16 [2, 256, 4096], P(None, 'dp'), may hold values from -6 to 6
- norm_gain: float32 [2, 4096], P('section'), may hold values from 0.1 to 1.9
- w_up: bfloat16 [2, 4096, 8192], P('section', 'dp', 'mp'), may hold values from -0.09375 to 0.09375
- w_down: bfloat16 [2, 4096, 8192], P('section', 'dp', 'mp'), may hold values from -0.0625 to 0.0625
- gram_left: float32 [2, 128, 512, 512], P('section', ('dp', 'mp')), as said below
- gram_right: float32 [2, 128, 512, 512], P('section', ('dp', 'mp')), as said below
- root_left: bfloat16 [2, 128, 512, 512], P('section', ('dp', 'mp'))
- root_right: bfloat16 [2, 128, 512, 512], P('section', ('dp', 'mp'))
- owner_slot: int32 [2, 16, 8], replicated, may hold values from 0 to 127, as said below
- eighth: int32 [2, 16, 8], replicated, may hold values from 0 to 7, as said below
- refresh_phase: int32 [1], replicated, may hold values from 0 to 999999
Outputs:
- new_gram_left: float32 [2, 128, 512, 512], P('section', ('dp', 'mp'))
- new_gram_right: float32 [2, 128, 512, 512], P('section', ('dp', 'mp'))
- new_root_left: bfloat16 [2, 128, 512, 512], P('section', ('dp', 'mp'))
- new_root_right: bfloat16 [2, 128, 512, 512], P('section', ('dp', 'mp'))
- update_blocks: bfloat16 [2, 128, 512, 512], P('section', ('dp', 'mp'))
Inputs may be any that keep to these rules, and one draw needn't show every extreme that they name: `owner_slot`: for each section, a permutation of the 128 slots; the block of flat index f = i * 8 + j goes to a slot t with (t // 8) % (4) == f // 32. `eighth`: in each section and each run of 32 consecutive flat block indices, every value is taken by exactly 4 blocks. `gram_left`: symmetric positive definite. `gram_right`: symmetric positive definite.
All inputs are finite; a program needn't handle non-finite values.
Results may differ from a plain program's by a relative error of at most 0.025.
Values may be sent and summed in bfloat16 or wider, within the bound.
A program may use at most 192 MiB of HBM per device.

v0:
```python
import math
import jax
import jax.numpy as jnp
from jax import lax
from jax.sharding import PartitionSpec as P

BLK = 512
ITERS = 2
norm_epsilon = 1e-05
decay_rate = 0.9
ridge_shift = 0.001
highest = lax.Precision.HIGHEST


def passed_along(block, axis, distance):
    devices = range(lax.axis_size(axis))
    route = [(i - distance, i) for i in devices if i - distance in devices]
    return lax.ppermute(block, axis, route)


def normalize_values(values, gain_row):
    inverse_rms = lax.rsqrt(jnp.mean(values * values, axis=-1, keepdims=True) + norm_epsilon)
    return values * inverse_rms * gain_row


def silu_slope(pre_act):
    sigmoid_values = jax.nn.sigmoid(pre_act)
    return sigmoid_values * (1.0 + pre_act * (1.0 - sigmoid_values))


def inverse_root(matrix):
    matrix_order = matrix.shape[-1]
    identity = jnp.eye(matrix_order, dtype=jnp.float32)
    shifted = matrix + ridge_shift * identity
    factor = 2.5 / jnp.sqrt(jnp.sum(shifted * shifted))
    iterate = jnp.power(factor, 0.25) * identity
    moment = factor * shifted
    for sweep_no in range(ITERS):
        step_mat = 1.25 * identity - 0.25 * moment
        square = jnp.dot(step_mat, step_mat, precision=highest)
        fourth = jnp.dot(square, square, precision=highest)
        moment = jnp.dot(fourth, moment, precision=highest)
        iterate = jnp.dot(iterate, step_mat, precision=highest)
    return iterate


def forward_layer(inputs, gain_row, up_rows, down_rows):
    values = inputs.astype(jnp.float32)
    normed = normalize_values(values, gain_row).astype(jnp.bfloat16)
    pre_act = jnp.dot(normed, up_rows, preferred_element_type=jnp.float32)
    hidden = jax.nn.silu(pre_act).astype(jnp.bfloat16)
    partial_value = lax.dot_general(
        hidden, down_rows, (((1,), (1,)), ((), ())), preferred_element_type=jnp.float32
    )
    branch = lax.psum(partial_value.astype(jnp.bfloat16), "mp").astype(jnp.float32)
    output = (values + branch).astype(jnp.bfloat16)
    return (output, pre_act, hidden)


def backward_layer(grad_output, inputs, pre_act, gain_row, up_rows, down_rows):
    grad_hidden = jnp.dot(grad_output, down_rows, preferred_element_type=jnp.float32)
    grad_pre = (grad_hidden * silu_slope(pre_act)).astype(jnp.bfloat16)
    partial_value = lax.dot_general(
        grad_pre, up_rows, (((1,), (1,)), ((), ())), preferred_element_type=jnp.float32
    )
    grad_normed = lax.psum(partial_value.astype(jnp.bfloat16), "mp").astype(jnp.float32)
    values = inputs.astype(jnp.float32)
    unused, pullback = jax.vjp(lambda values_in: normalize_values(values_in, gain_row), values)
    grad_values = pullback(grad_normed)[0]
    return (grad_output.astype(jnp.float32) + grad_values).astype(jnp.bfloat16)


def store_row(stack, entry, slot_index, is_valid):
    return jnp.where(is_valid, lax.dynamic_update_index_in_dim(stack, entry, slot_index, 0), stack)


def on_device(
    activations,
    cotangent,
    norm_gain,
    w_up,
    w_down,
    gram_left,
    gram_right,
    root_left,
    root_right,
    owner_slot,
    eighth,
    refresh_phase,
):
    section_no = lax.axis_index("section")
    dp_no = lax.axis_index("dp")
    mp_no = lax.axis_index("mp")
    section_total = lax.axis_size("section")
    dp_count = lax.axis_size("dp")
    mp_count = lax.axis_size("mp")
    micro_count, row_count, model_width = activations.shape
    gain_row = norm_gain[0]
    up_full, down_full = (
        lax.all_gather(w_up[0], "dp", axis=0, tiled=True),
        lax.all_gather(w_down[0], "dp", axis=0, tiled=True),
    )
    shard_ff = up_full.shape[1]
    tick_total = micro_count + section_total - 1
    inputs_all = jnp.zeros((micro_count, row_count, model_width), jnp.bfloat16)
    pre_all = jnp.zeros((micro_count, row_count, shard_ff), jnp.float32)
    hidden_all = jnp.zeros((micro_count, row_count, shard_ff), jnp.bfloat16)
    received = jnp.zeros((row_count, model_width), jnp.bfloat16)
    is_first = section_no == 0
    for tick_no in range(tick_total):
        batch_no = tick_no - section_no
        is_valid = (batch_no >= 0) & (batch_no < micro_count)
        slot_index = jnp.clip(batch_no, 0, micro_count - 1)
        inputs = jnp.where(is_first, activations[min(tick_no, micro_count - 1)], received)
        output, pre_act, hidden = forward_layer(inputs, gain_row, up_full, down_full)
        inputs_all = store_row(inputs_all, inputs, slot_index, is_valid)
        pre_all = store_row(pre_all, pre_act, slot_index, is_valid)
        hidden_all = store_row(hidden_all, hidden, slot_index, is_valid)
        if tick_no < tick_total - 1:
            received = passed_along(output, "section", 1)
    grad_all = jnp.zeros((micro_count, row_count, model_width), jnp.bfloat16)
    received = jnp.zeros((row_count, model_width), jnp.bfloat16)
    is_last = section_no == section_total - 1
    for tick_no in range(tick_total):
        batch_no = tick_no - (section_total - 1 - section_no)
        is_valid = (batch_no >= 0) & (batch_no < micro_count)
        slot_index = jnp.clip(batch_no, 0, micro_count - 1)
        grad_output = jnp.where(is_last, cotangent[min(tick_no, micro_count - 1)], received)
        inputs = lax.dynamic_index_in_dim(inputs_all, slot_index, 0, keepdims=False)
        pre_act = lax.dynamic_index_in_dim(pre_all, slot_index, 0, keepdims=False)
        grad_all = store_row(grad_all, grad_output, slot_index, is_valid)
        grad_input = backward_layer(grad_output, inputs, pre_act, gain_row, up_full, down_full)
        if tick_no < tick_total - 1:
            received = passed_along(grad_input, "section", -1)
    token_count = micro_count * row_count
    block_rows = shard_ff // BLK
    block_cols = model_width // BLK
    group_size = block_rows * block_cols
    per_dev = group_size // dp_count
    hidden_flat = hidden_all.reshape(token_count, block_rows, BLK)
    grad_flat = grad_all.reshape(token_count, block_cols, BLK)
    section_owner = lax.dynamic_index_in_dim(owner_slot, section_no, 0, keepdims=False)
    local_owner = lax.dynamic_slice_in_dim(
        section_owner, mp_no * block_rows, block_rows, 0
    ).reshape(-1)
    local_slot = local_owner // (mp_count * per_dev) * per_dev + local_owner % per_dev
    block_of_slot = jnp.argsort(local_slot)
    row_of_slot = block_of_slot // block_cols
    col_of_slot = block_of_slot % block_cols
    hidden_slots = jnp.take(hidden_flat, row_of_slot, axis=1)
    grad_slots = jnp.take(grad_flat, col_of_slot, axis=1)
    hidden_recv, grad_recv = (
        lax.all_to_all(hidden_slots, "dp", split_axis=1, concat_axis=0, tiled=True),
        lax.all_to_all(grad_slots, "dp", split_axis=1, concat_axis=0, tiled=True),
    )
    hidden_in = hidden_recv.reshape(dp_count, token_count, per_dev, BLK)
    grad_in = grad_recv.reshape(dp_count, token_count, per_dev, BLK)
    products = jnp.einsum("snbk,snbl->sbkl", hidden_in, grad_in, preferred_element_type=jnp.float32)
    rounded = lax.optimization_barrier(products.astype(jnp.bfloat16)).astype(jnp.float32)
    summed = jnp.sum(rounded, axis=0)
    scaled = summed * (1.0 / math.sqrt(token_count * dp_count))
    left_new = (
        decay_rate * gram_left[0]
        + jnp.einsum("sij,skj->sik", scaled, scaled, precision=highest) / BLK
    )
    right_new = (
        decay_rate * gram_right[0]
        + jnp.einsum("sji,sjk->sik", scaled, scaled, precision=highest) / BLK
    )
    phase_now = refresh_phase[0] % 8
    section_eighth = lax.dynamic_index_in_dim(eighth, section_no, 0, keepdims=False)
    local_eighth = lax.dynamic_slice_in_dim(
        section_eighth, mp_no * block_rows, block_rows, 0
    ).reshape(-1)
    is_due = jnp.take(local_eighth, block_of_slot) == phase_now
    my_due = lax.dynamic_slice_in_dim(is_due, dp_no * per_dev, per_dev)

    def refresh_slot(operands):
        return lax.cond(
            operands[0],
            lambda ops: (
                inverse_root(ops[1]).astype(jnp.bfloat16),
                inverse_root(ops[2]).astype(jnp.bfloat16),
            ),
            lambda ops: (ops[3], ops[4]),
            operands,
        )

    roots_l, roots_r = lax.map(
        refresh_slot, (my_due, left_new, right_new, root_left[0], root_right[0])
    )
    grad_low = scaled.astype(jnp.bfloat16)
    inner_product = jnp.einsum(
        "sij,sjk->sik", grad_low, roots_r, preferred_element_type=jnp.float32
    ).astype(jnp.bfloat16)
    update = jnp.einsum(
        "sij,sjk->sik", roots_l, inner_product, preferred_element_type=jnp.float32
    ).astype(jnp.bfloat16)
    return (left_new[None], right_new[None], roots_l[None], roots_r[None], update[None])


def solution(mesh):
    return jax.shard_map(
        on_device,
        mesh=mesh,
        in_specs=(
            P(None, "dp", None),
            P(None, "dp", None),
            P("section", None),
            P("section", "dp", "mp"),
            P("section", "dp", "mp"),
            P("section", ("dp", "mp"), None, None),
            P("section", ("dp", "mp"), None, None),
            P("section", ("dp", "mp"), None, None),
            P("section", ("dp", "mp"), None, None),
            P(),
            P(),
            P(),
        ),
        out_specs=(
            P("section", ("dp", "mp"), None, None),
            P("section", ("dp", "mp"), None, None),
            P("section", ("dp", "mp"), None, None),
            P("section", ("dp", "mp"), None, None),
            P("section", ("dp", "mp"), None, None),
        ),
        check_vma=False,
    )
```

profile of v0, /device:TPU:0, one launch (start us, length us, event | category | flops | bytes accessed | tf_op | source)
XLA Modules:
  0.0 786.2 jit_solution(6627781290026587765)
XLA Ops:
  9.0 109.2 %all-gather.5.cloned.1.call-done = bf16[1,4096,2048]{2,1,0:T(8,128)(2,1)} async-done(((bf16[1,1024,2048]{2,1,0:T(8,128)(2,1)}), bf16[1,4096,2048]{2,1,0:T(8,128)(2,1)}) %all-gather.5.cloned.1.call-update) | async-done | bytes 16777232 | tf_op jit(solution)/shard_map/all_gather | solution.py:100
  118.3 8.9 %bitcast_dynamic-update-slice_fusion.1 = (bf16[2,64,2048]{2,1,0:T(8,128)(2,1)S(1)}, f32[64,2048]{1,0:T(8,128)S(1)}) fusion(bf16[2,64,2048]{2,1,0:T(8,128)(2,1)S(1)} %broadcast_in_dim.113, s32[]{:T(128)S(6)} %min.19, pred[]{:T(512)S(6)} %and.63, bf16[1,4096,2048]{2,1,0:T(8,128)(2,1)} %all-gather.5.cloned.1.call-done, f32[4096]{0:T(1024)S(1)} %bitcast.238, ...), kind=kOutput, calls=%fused_computation.236 | convolution fusion | flops 1075838976 | bytes 18104838 | tf_op jit(solution)/shard_map/dot_general | solution.py:50
  127.2 98.5 %all-gather.7.cloned.1.call-done = bf16[1,4096,2048]{2,1,0:T(8,128)(2,1)} async-done(((bf16[1,1024,2048]{2,1,0:T(8,128)(2,1)}), bf16[1,4096,2048]{2,1,0:T(8,128)(2,1)}) %all-gather.7.cloned.1.call-update) | async-done | bytes 16777232 | tf_op jit(solution)/shard_map/all_gather | solution.py:101
  225.7 11.7 %fusion.108 = bf16[64,4096]{1,0:T(8,128)(2,1)} fusion(bf16[1,4096,2048]{2,1,0:T(8,128)(2,1)} %all-gather.7.cloned.1.call-done, f32[64,2048]{1,0:T(8,128)S(1)} %get-tuple-element.165), kind=kOutput, calls=%fused_computation.130 | convolution fusion | flops 1074659328 | bytes 17825792 | tf_op jit(solution)/shard_map/dot_general | solution.py:52
  237.5 38.7 %all-reduce.5.cloned.1.call-done = bf16[64,4096]{1,0:T(8,128)(2,1)} async-done(((bf16[64,4096]{1,0:T(8,128)(2,1)}), bf16[64,4096]{1,0:T(8,128)(2,1)}) %all-reduce.5.cloned.1.call-update) | async-done | bytes 524304 | tf_op jit(solution)/shard_map/psum | solution.py:55
  277.4 3.6 collective-permute-start
  281.3 9.8 %collective-permute-done = bf16[64,4096]{1,0:T(8,128)(2,1)S(1)} collective-permute-done((bf16[64,4096]{1,0:T(8,128)(2,1)S(1)}, bf16[64,4096]{1,0:T(8,128)(2,1)S(1)}, u32[]{:S(2)}, u32[]{:S(2)}) %collective-permute-start) | collective-permute-done | bytes 524320 | tf_op jit(solution)/shard_map/ppermute | solution.py:18
  291.6 9.7 %fusion.198 = (bf16[2,64,2048]{2,1,0:T(8,128)(2,1)S(1)}, f32[64,2048]{1,0:T(8,128)}) fusion(bf16[2,64,2048]{2,1,0:T(8,128)(2,1)S(1)} %get-tuple-element.164, s32[]{:T(128)S(6)} %min.20, pred[]{:T(512)S(6)} %and.64, bf16[1,4096,2048]{2,1,0:T(8,128)(2,1)} %all-gather.5.cloned.1.call-done, bf16[64,4096]{1,0:T(8,128)(2,1)S(1)} %get-tuple-element.148, ...), kind=kOutput, calls=%fused_computation.235 | convolution fusion | flops 1075576832 | bytes 18366980 | tf_op jit(solution)/shard_map/dot_general | solution.py:50
  301.3 12.1 %fusion.111 = bf16[64,4096]{1,0:T(8,128)(2,1)} fusion(bf16[1,4096,2048]{2,1,0:T(8,128)(2,1)} %all-gather.7.cloned.1.call-done, f32[64,2048]{1,0:T(8,128)} %get-tuple-element.167), kind=kOutput, calls=%fused_computation.131 | convolution fusion | flops 1074659328 | bytes 17825792 | tf_op jit(solution)/shard_map/dot_general | solution.py:52
  316.2 36.6 %all-reduce.7.cloned.1.call-done = bf16[64,4096]{1,0:T(8,128)(2,1)} async-done(((bf16[64,4096]{1,0:T(8,128)(2,1)}), bf16[64,4096]{1,0:T(8,128)(2,1)}) %all-reduce.7.cloned.1.call-update) | async-done | bytes 524304 | tf_op jit(solution)/shard_map/psum | solution.py:55
  354.0 3.7 collective-permute-start.1
  362.7 5.0 collective-permute-done.1
  368.1 9.0 %fusion.197 = (bf16[2,64,2048]{2,1,0:T(8,128)(2,1)S(1)}, f32[64,2048]{1,0:T(8,128)S(1)}) fusion(bf16[2,64,2048]{2,1,0:T(8,128)(2,1)S(1)} %copy-done.4, s32[]{:T(128)S(6)} %min.21, pred[]{:T(512)S(6)} %and.65, bf16[1,4096,2048]{2,1,0:T(8,128)(2,1)} %all-gather.5.cloned.1.call-done, bf16[64,4096]{1,0:T(8,128)(2,1)S(1)} %get-tuple-element.146, ...), kind=kOutput, calls=%fused_computation.233 | convolution fusion | flops 1075576832 | bytes 18366980 | tf_op jit(solution)/shard_map/dot_general | solution.py:50
  379.9 15.7 %fusion.102 = bf16[64,4096]{1,0:T(8,128)(2,1)} fusion(bf16[1,4096,2048]{2,1,0:T(8,128)(2,1)} %all-gather.5.cloned.1.call-done, bf16[1,4096,2048]{2,1,0:T(8,128)(2,1)} %all-gather.7.cloned.1.call-done, f32[2,64,2048]{2,1,0:T(8,128)} %fusion.180, s32[]{:T(128)S(6)} %min.22, bf16[2,64,4096]{2,1,0:T(8,128)(2,1)S(1)} %copy-done.2, pred[]{:T(512)S(6)} %eq.60), kind=kOutput, calls=%fused_computation.128 | convolution fusion | flops 2149187584 | bytes 35127300 | tf_op jit(solution)/shard_map/dot_general | solution.py:63
  397.6 37.3 %all-reduce.9.cloned.1.call-done = bf16[64,4096]{1,0:T(8,128)(2,1)} async-done(((bf16[64,4096]{1,0:T(8,128)(2,1)}), bf16[64,4096]{1,0:T(8,128)(2,1)}) %all-reduce.9.cloned.1.call-update) | async-done | bytes 524304 | tf_op jit(solution)/shard_map/psum | solution.py:66
  440.4 12.2 %collective-permute-done.2 = bf16[64,4096]{1,0:T(8,128)(2,1)} collective-permute-done((bf16[64,4096]{1,0:T(8,128)(2,1)S(1)}, bf16[64,4096]{1,0:T(8,128)(2,1)}, u32[]{:S(2)}, u32[]{:S(2)}) %collective-permute-start.2) | collective-permute-done | bytes 524320 | tf_op jit(solution)/shard_map/ppermute | solution.py:18
  454.9 15.8 %fusion.105 = bf16[64,4096]{1,0:T(8,128)(2,1)} fusion(bf16[1,4096,2048]{2,1,0:T(8,128)(2,1)} %all-gather.5.cloned.1.call-done, bf16[64,4096]{1,0:T(8,128)(2,1)S(1)} %get-tuple-element.144, bf16[1,4096,2048]{2,1,0:T(8,128)(2,1)} %all-gather.7.cloned.1.call-done, f32[2,64,2048]{2,1,0:T(8,128)} %fusion.180, s32[]{:T(128)S(6)} %min.23), kind=kOutput, calls=%fused_computation.129 | convolution fusion | flops 2148925440 | bytes 35127300 | tf_op jit(solution)/shard_map/dot_general | solution.py:63
  475.8 4.7 select_bitcast_fusion.1
  480.5 4.8 all-to-all-start
  485.4 22.8 %all-reduce.11.cloned.1.call-done = bf16[64,4096]{1,0:T(8,128)(2,1)} async-done(((bf16[64,4096]{1,0:T(8,128)(2,1)}), bf16[64,4096]{1,0:T(8,128)(2,1)}) %all-reduce.11.cloned.1.call-update) | async-done | bytes 524304 | tf_op jit(solution)/shard_map/psum | solution.py:66
  512.2 13.3 %collective-permute-done.3 = bf16[64,4096]{1,0:T(8,128)(2,1)S(1)} collective-permute-done((bf16[64,4096]{1,0:T(8,128)(2,1)S(1)}, bf16[64,4096]{1,0:T(8,128)(2,1)S(1)}, u32[]{:S(2)}, u32[]{:S(2)}) %collective-permute-start.3) | collective-permute-done | bytes 524320 | tf_op jit(solution)/shard_map/ppermute | solution.py:18
  532.3 4.7 select_bitcast_fusion
  537.0 5.0 all-to-all-start.1
  542.1 6.4 copy.34
  548.6 41.7 %all-to-all-done.1 = bf16[128,32,512]{2,0,1:T(8,128)(2,1)} async-done(((bf16[128,32,512]{2,0,1:T(8,128)(2,1)}), bf16[128,32,512]{2,0,1:T(8,128)(2,1)}, u32[]{:S(2)}, u32[]{:S(2)}) %all-to-all-start.1) | async-done | bytes 4194336 | tf_op jit(solution)/shard_map/all_to_all | solution.py:154
  590.2 10.9 %convolution_convert_fusion.2 = bf16[4,8,512,512]{3,2,1,0:T(8,128)(2,1)} fusion(bf16[4,128,8,512]{1,3,2,0:T(8,128)(2,1)} %bitcast.236, bf16[4,128,8,512]{3,1,2,0:T(8,128)(2,1)} %bitcast.37), kind=kOutput, calls=%fused_computation.120 | convolution fusion | flops 2155872256 | bytes 25165824 | tf_op jit(solution)/shard_map/snbk,snbl->sbkl/dot_general | solution.py:158
  601.1 9.6 %convert_reduce_fusion = f32[8,512,512]{2,1,0:T(8,128)S(1)} fusion(bf16[4,8,512,512]{3,2,1,0:T(8,128)(2,1)} %convolution_convert_fusion.2), kind=kLoop, calls=%fused_computation.101 | loop fusion | flops 14680064 | bytes 25165824 | tf_op jit(solution)/shard_map/reduce_sum | solution.py:160
  610.7 19.7 %bitcast_add_fusion = f32[8,512,512]{2,1,0:T(8,128)} fusion(f32[1,8,512,512]{3,2,1,0:T(8,128)} %param.22, f32[8,512,512]{2,1,0:T(8,128)S(1)} %convert_reduce_fusion), kind=kOutput, calls=%fused_computation.121 | convolution fusion | flops 12893290496 | bytes 25165824 | tf_op jit(solution)/shard_map/sji,sjk->sik/dot_general | solution.py:168
  630.4 17.6 %bitcast_add_fusion.1 = f32[8,512,512]{2,1,0:T(8,128)} fusion(f32[1,8,512,512]{3,2,1,0:T(8,128)} %param.21, f32[8,512,512]{2,1,0:T(8,128)S(1)} %convert_reduce_fusion), kind=kOutput, calls=%fused_computation.122 | convolution fusion | flops 12893290496 | bytes 25165824 | tf_op jit(solution)/shard_map/sij,skj->sik/dot_general | solution.py:164
  648.0 118.6 %while.12 = (s32[]{:T(128)}, bf16[8,512,512]{2,1,0:T(8,128)(2,1)}, bf16[8,512,512]{2,1,0:T(8,128)(2,1)}, pred[8]{0:T(512)(128)(4,1)S(1)}, bf16[8,512,512]{2,1,0:...) while((s32[]{:T(128)}, bf16[8,512,512]{2,1,0:T(8,128)(2,1)}, ...), condition=%wide.region_18.19_spmd, body=%wide.region_13.18_spmd.sunk | while | flops 16121331712 | bytes 28315412 | solution.py:189
  660.1 31.2 %conditional.2 = (bf16[1,512,512]{2,1,0:T(8,128)(2,1)S(1)}, bf16[1,512,512]{2,1,0:T(8,128)(2,1)S(1)}) conditional(s32[]{:T(128)} %bitcast.230, (bf16[8,512,512]{2,1,0:T(8,128)(2,1)}, s32[]{:T(128)}, bf16[8,512,512]{2,1,0:T(8,128)(2,1)}) %tuple.65, (f32[8,512,512]{2,1,0:T(8,128)}, s32[]{:T(128)}, f32[8,512,512]{2,1,0:T(8,128)}) %tuple.66), branch_computations={%region_14.14_spmd, %region_15.17_spmd} | conditional | flops 16121331712 | bytes 26217596 | solution.py:179
  663.3 3.6 fusion.6
  668.8 3.1 select_subtract_fusion
  677.7 3.7 fusion.3
  683.2 3.1 select_subtract_fusion.2
  686.4 3.1 fusion.14
  693.6 31.1 %conditional.2 = (bf16[1,512,512]{2,1,0:T(8,128)(2,1)S(1)}, bf16[1,512,512]{2,1,0:T(8,128)(2,1)S(1)}) conditional(s32[]{:T(128)} %bitcast.230, (bf16[8,512,512]{2,1,0:T(8,128)(2,1)}, s32[]{:T(128)}, bf16[8,512,512]{2,1,0:T(8,128)(2,1)}) %tuple.65, (f32[8,512,512]{2,1,0:T(8,128)}, s32[]{:T(128)}, f32[8,512,512]{2,1,0:T(8,128)}) %tuple.66), branch_computations={%region_14.14_spmd, %region_15.17_spmd} | conditional | flops 16121331712 | bytes 26217596 | solution.py:179
  696.8 3.6 fusion.6
  702.3 3.1 select_subtract_fusion
  711.1 3.6 fusion.3
  716.6 3.1 select_subtract_fusion.2
  727.1 31.1 %conditional.2 = (bf16[1,512,512]{2,1,0:T(8,128)(2,1)S(1)}, bf16[1,512,512]{2,1,0:T(8,128)(2,1)S(1)}) conditional(s32[]{:T(128)} %bitcast.230, (bf16[8,512,512]{2,1,0:T(8,128)(2,1)}, s32[]{:T(128)}, bf16[8,512,512]{2,1,0:T(8,128)(2,1)}) %tuple.65, (f32[8,512,512]{2,1,0:T(8,128)}, s32[]{:T(128)}, f32[8,512,512]{2,1,0:T(8,128)}) %tuple.66), branch_computations={%region_14.14_spmd, %region_15.17_spmd} | conditional | flops 16121331712 | bytes 26217596 | solution.py:179
  730.2 3.6 fusion.6
  735.7 3.1 select_subtract_fusion
  744.5 3.6 fusion.3
  750.0 3.1 select_subtract_fusion.2
  753.2 3.1 fusion.14
  766.6 12.3 %convert_bitcast_fusion = bf16[1,8,512,512]{3,2,1,0:T(8,128)(2,1)} fusion(bf16[8,512,512]{2,1,0:T(8,128)(2,1)} %get-tuple-element.120, bf16[8,512,512]{2,1,0:T(8,128)(2,1)} %get-tuple-element.121, f32[8,512,512]{2,1,0:T(8,128)} %copy-done), kind=kOutput, calls=%fused_computation.135 | convolution fusion | flops 4303355904 | bytes 20971520 | tf_op jit(solution)/shard_map/sij,sjk->sik/dot_general | solution.py:196
  (132 shorter events, 108.8 us)
Async XLA Ops:
  7.2 1.6 copy-start.1
  7.2 111.1 %copy-start.8 = (f32[1,4096]{1,0:T(1,128)S(1)}, f32[1,4096]{1,0:T(1,128)}, u32[]{:S(2)}) copy-start(f32[1,4096]{1,0:T(1,128)} %param.18) | copy-start | bytes 49156
  7.2 111.0 %all-gather.5.cloned.1.call-start = ((), (), s32[]{:S(2)}) async-start(), calls=%async_computation.6 | async-start | bytes 20971520 | tf_op jit(solution)/shard_map/all_gather | solution.py:100
  7.9 217.8 %all-gather.7.cloned.1.call-start = ((), (), s32[]{:S(2)}) async-start(), calls=%async_computation.7 | async-start | bytes 20971520 | tf_op jit(solution)/shard_map/all_gather | solution.py:101
  8.7 267.6 %all-reduce.5.cloned.1.call-start = ((), (), s32[]{:S(2)}) async-start(), calls=%async_computation.2 | async-start | bytes 1048576 | tf_op jit(solution)/shard_map/psum | solution.py:55
  127.2 110.2 %copy-start.7 = (f32[64,2048]{1,0:T(8,128)}, f32[64,2048]{1,0:T(8,128)S(1)}, u32[]{:S(2)}) copy-start(f32[64,2048]{1,0:T(8,128)S(1)} %get-tuple-element.165) | copy-start | bytes 1572868
  237.5 115.3 %all-reduce.7.cloned.1.call-start = ((), (), s32[]{:S(2)}) async-start(), calls=%async_computation.3 | async-start | bytes 1048576 | tf_op jit(solution)/shard_map/psum | solution.py:55
  277.4 13.6 %collective-permute-start = (bf16[64,4096]{1,0:T(8,128)(2,1)S(1)}, bf16[64,4096]{1,0:T(8,128)(2,1)S(1)}, u32[]{:S(2)}, u32[]{:S(2)}) collective-permute-start(bf16[64,4096]{1,0:T(8,128)(2,1)S(1)} %fusion.152), channel_id=1, source_target_pairs={{0,16},{1,17},{2,18},{3,19},{4,20},{5,21},{6,22},{7,23},{8,24},{9,... | collective-permute-start | bytes 1572872 | tf_op jit(solution)/shard_map/ppermute | solution.py:18
  301.3 13.2 %copy-start.3 = (bf16[2,64,2048]{2,1,0:T(8,128)(2,1)}, bf16[2,64,2048]{2,1,0:T(8,128)(2,1)S(1)}, u32[]{:S(2)}) copy-start(bf16[2,64,2048]{2,1,0:T(8,128)(2,1)S(1)} %get-tuple-element.166) | copy-start | bytes 1572868
  301.3 12.9 %copy-start.9 = (s32[2,16,8]{1,2,0:T(8,128)S(1)}, s32[2,16,8]{1,2,0:T(8,128)}, u32[]{:S(2)}) copy-start(s32[2,16,8]{1,2,0:T(8,128)} %param.26) | copy-start | bytes 3076
  301.3 12.9 %copy-start.10 = (s32[2,16,8]{1,2,0:T(8,128)S(1)}, s32[2,16,8]{1,2,0:T(8,128)}, u32[]{:S(2)}) copy-start(s32[2,16,8]{1,2,0:T(8,128)} %param.25) | copy-start | bytes 3076
  313.4 121.6 %all-reduce.9.cloned.1.call-start = ((), (), s32[]{:S(2)}) async-start(), calls=%async_computation.4 | async-start | bytes 1048576 | tf_op jit(solution)/shard_map/psum | solution.py:66
  352.8 15.3 %copy-start.4 = (bf16[2,64,2048]{2,1,0:T(8,128)(2,1)S(1)}, bf16[2,64,2048]{2,1,0:T(8,128)(2,1)}, u32[]{:S(2)}) copy-start(bf16[2,64,2048]{2,1,0:T(8,128)(2,1)} %copy-done.3) | copy-start | bytes 1572868
  354.0 13.6 %collective-permute-start.1 = (bf16[64,4096]{1,0:T(8,128)(2,1)S(1)}, bf16[64,4096]{1,0:T(8,128)(2,1)S(1)}, u32[]{:S(2)}, u32[]{:S(2)}) collective-permute-start(bf16[64,4096]{1,0:T(8,128)(2,1)S(1)} %fusion.144), channel_id=1, source_target_pairs={{0,16},{1,17},{2,18},{3,19},{4,20},{5,21},{6,22},{7,23},{8,24},{9,... | collective-permute-start | bytes 1572872 | tf_op jit(solution)/shard_map/ppermute | solution.py:18
  368.1 11.7 %copy-start.2 = (bf16[2,64,4096]{2,1,0:T(8,128)(2,1)S(1)}, bf16[2,64,4096]{2,1,0:T(8,128)(2,1)}, u32[]{:S(2)}) copy-start(bf16[2,64,4096]{2,1,0:T(8,128)(2,1)} %param.17) | copy-start | bytes 3145732
  377.2 0.8 copy-start.5
  395.6 112.6 %all-reduce.11.cloned.1.call-start = ((), (), s32[]{:S(2)}) async-start(), calls=%async_computation.5 | async-start | bytes 1048576 | tf_op jit(solution)/shard_map/psum | solution.py:66
  437.9 14.7 %collective-permute-start.2 = (bf16[64,4096]{1,0:T(8,128)(2,1)S(1)}, bf16[64,4096]{1,0:T(8,128)(2,1)}, u32[]{:S(2)}, u32[]{:S(2)}) collective-permute-start(bf16[64,4096]{1,0:T(8,128)(2,1)S(1)} %fusion.146), channel_id=1, source_target_pairs={{16,0},{17,1},{18,2},{19,3},{20,4},{21,5},{22,6},{23,7},{24,8},{25... | collective-permute-start | bytes 1572872 | tf_op jit(solution)/shard_map/ppermute | solution.py:18
  454.9 15.8 %copy-start.6 = (bf16[2,64,2048]{2,1,0:T(8,128)(2,1)S(1)}, bf16[2,64,2048]{2,1,0:T(8,128)(2,1)}, u32[]{:S(2)}) copy-start(bf16[2,64,2048]{2,1,0:T(8,128)(2,1)} %copy-done.5) | copy-start | bytes 1572868
  480.5 56.5 %all-to-all-start = ((bf16[128,32,512]{2,0,1:T(8,128)(2,1)}), bf16[128,32,512]{2,0,1:T(8,128)(2,1)}, u32[]{:S(2)}, u32[]{:S(2)}) async-start(bf16[128,32,512]{2,0,1:T(8,128)(2,1)} %select_bitcast_fusion.1), calls=%async_computation | async-start | bytes 8388608 | tf_op jit(solution)/shard_map/all_to_all | solution.py:153
  510.9 14.6 %collective-permute-start.3 = (bf16[64,4096]{1,0:T(8,128)(2,1)S(1)}, bf16[64,4096]{1,0:T(8,128)(2,1)S(1)}, u32[]{:S(2)}, u32[]{:S(2)}) collective-permute-start(bf16[64,4096]{1,0:T(8,128)(2,1)S(1)} %fusion.148), channel_id=1, source_target_pairs={{16,0},{17,1},{18,2},{19,3},{20,4},{21,5},{22,6},{23,7},{24,8},{25... | collective-permute-start | bytes 1572872 | tf_op jit(solution)/shard_map/ppermute | solution.py:18
  537.0 53.2 %all-to-all-start.1 = ((bf16[128,32,512]{2,0,1:T(8,128)(2,1)}), bf16[128,32,512]{2,0,1:T(8,128)(2,1)}, u32[]{:S(2)}, u32[]{:S(2)}) async-start(bf16[128,32,512]{2,0,1:T(8,128)(2,1)} %select_bitcast_fusion), calls=%async_computation.1 | async-start | bytes 8388608 | tf_op jit(solution)/shard_map/all_to_all | solution.py:154
  610.7 19.7 %copy-start = (f32[8,512,512]{2,1,0:T(8,128)}, f32[8,512,512]{2,1,0:T(8,128)S(1)}, u32[]{:S(2)}) copy-start(f32[8,512,512]{2,1,0:T(8,128)S(1)} %convert_reduce_fusion) | copy-start | bytes 25165828
Sparse Core Ops, SparseCore 0:
  9.5 108.6 all-gather.4
  119.8 105.8 all-gather.6
  237.6 38.6 all-reduce.4
  313.5 39.2 all-reduce.6
  395.7 39.1 all-reduce.8
  470.8 37.3 all-reduce.10
where the time goes:
time: 794 us; the launch traced here: 786 us
  waiting for transfers between devices  427 us (54%)
  matrix products  225 us (28%)
  other arithmetic  48.4 us (6%)
  local copies, waits for them, and re-layouts  40 us (5%)
  starting transfers between devices  20.4 us (3%)
  between operations  15.6 us (2%)
  loops' own time  10.5 us (1%)
    all_gather x1, waiting for transfers between devices, on_device(): lax.all_gather(w_up[0], 'dp', axis=0, tiled=True)  109 us
    all_gather x1, waiting for transfers between devices, on_device(): lax.all_gather(w_down[0], 'dp', axis=0, tiled=True)  98.5 us
    psum x2, waiting for transfers between devices, forward_layer(): lax.psum(partial_value.astype(jnp.bfloat16), 'mp').astype(jnp.float32)  75.3 us
    psum x2, waiting for transfers between devices, backward_layer(): lax.psum(partial_value.astype(jnp.bfloat16), 'mp').astype(jnp.float32)  60.1 us
    all_to_all x1, waiting for transfers between devices, on_device(): lax.all_to_all(grad_slots, 'dp', split_axis=1, concat_axis=0, tiled=True)  41.7 us
    ppermute x4, waiting for transfers between devices, passed_along(): return lax.ppermute(block, axis, route)  40.3 us
    dot_general x2, matrix products, backward_layer(): lax.dot_general(grad_pre, up_rows, (((1,), (1,)), ((), ())), preferred_el...  31.5 us
    dot_general x12, matrix products, inverse_root(): iterate = jnp.dot(iterate, step_mat, precision=highest)  29.8 us
  transfers between devices with their start and end apart: 12, of which 11 were waited for; matrix products, arithmetic and copies ran while one was open for 6% of the time, Pallas kernels for 0%

commit v1 on v0

--- a/solution.py
+++ b/solution.py
@@ -10,6 +10,27 @@
 decay_rate = 0.9
 ridge_shift = 0.001
 highest = lax.Precision.HIGHEST
+
+
+def in_order(tiles, dim):
+    dims = list(tiles.shape[1:])
+    dims[dim] *= tiles.shape[0]
+    return jnp.moveaxis(tiles, 0, dim).reshape(dims)
+
+
+def grow_blocks(value, axis):
+    count, index = (lax.axis_size(axis), lax.axis_index(axis))
+    pieces, apart = (value[None], 1)
+    while apart < count:
+        other = lax.ppermute(pieces, axis, [(i, i ^ apart) for i in range(count)])
+        low = index & apart == 0
+        pieces = jnp.concatenate([jnp.where(low, pieces, other), jnp.where(low, other, pieces)])
+        apart *= 2
+    return pieces
+
+
+def doubled_up(x, axis, dim):
+    return in_order(grow_blocks(x, axis), dim)
 
 
 def passed_along(block, axis, distance):
@@ -97,7 +118,7 @@
     micro_count, row_count, model_width = activations.shape
     gain_row = norm_gain[0]
     up_full, down_full = (
-        lax.all_gather(w_up[0], "dp", axis=0, tiled=True),
+        doubled_up(w_up[0], "dp", 0),
         lax.all_gather(w_down[0], "dp", axis=0, tiled=True),
     )
     shard_ff = up_full.shape[1]

time: 794 us -> 883 us (1.11)
  waiting for transfers between devices: 427 us -> 487 us
  other arithmetic: 48.4 us -> 71.7 us
    ppermute x0 -> x2, waiting for transfers between devices: none -> 269 us  [grow_blocks(): other = lax.ppermute(pieces, axis, [(i, i ^ apart) for i in range(count)])]
    all_gather x1 -> x0, waiting for transfers between devices: 109 us -> none  [on_device(): lax.all_gather(w_up[0], 'dp', axis=0, tiled=True)]
    all_gather x1, waiting for transfers between devices: 98.5 us -> 0.02 us  [on_device(): lax.all_gather(w_down[0], 'dp', axis=0, tiled=True)]
    select_n x0 -> x2, other arithmetic: none -> 12.6 us  [grow_blocks(): jnp.where(low, pieces, other)]
    concatenate x0 -> x2, other arithmetic: none -> 10.7 us  [grow_blocks(): jnp.concatenate([jnp.where(low, pieces, other), jnp.where(low, other, pie...]
  transfers between devices with their start and end apart: 12 -> 13, of which waited for: 11 -> 11; matrix products, arithmetic and copies ran while one was open for 6% -> 8% of each run, Pallas kernels for 0% -> 0%
where the time goes in v1:
time: 883 us; the launch traced here: 874 us
  waiting for transfers between devices  487 us (55%)
  matrix products  220 us (25%)
  other arithmetic  71.7 us (8%)
  local copies, waits for them, and re-layouts  45.7 us (5%)
  starting transfers between devices  24 us (3%)
  between operations  15.3 us (2%)
  loops' own time  10.4 us (1%)
    ppermute x2, waiting for transfers between devices, grow_blocks(): other = lax.ppermute(pieces, axis, [(i, i ^ apart) for i in range(count)])  269 us
    psum x2, waiting for transfers between devices, forward_layer(): lax.psum(partial_value.astype(jnp.bfloat16), 'mp').astype(jnp.float32)  75.3 us
    psum x2, waiting for transfers between devices, backward_layer(): lax.psum(partial_value.astype(jnp.bfloat16), 'mp').astype(jnp.float32)  60.2 us
    all_to_all x1, waiting for transfers between devices, on_device(): lax.all_to_all(grad_slots, 'dp', split_axis=1, concat_axis=0, tiled=True)  41.7 us
    ppermute x4, waiting for transfers between devices, passed_along(): return lax.ppermute(block, axis, route)  40.3 us
    dot_general x2, matrix products, backward_layer(): lax.dot_general(grad_pre, up_rows, (((1,), (1,)), ((), ())), preferred_el...  31.5 us
    dot_general x12, matrix products, inverse_root(): iterate = jnp.dot(iterate, step_mat, precision=highest)  29.8 us
    dot_general x2, matrix products, forward_layer(): lax.dot_general(hidden, down_rows, (((1,), (1,)), ((), ())), preferred_el...  24.1 us
  transfers between devices with their start and end apart: 13, of which 11 were waited for; matrix products, arithmetic and copies ran while one was open for 8% of the time, Pallas kernels for 0%

profile of v1, /device:TPU:0, one launch (start us, length us, event | category | flops | bytes accessed | tf_op | source)
XLA Modules:
  0.0 874.4 jit_solution(6871640006053946199)
XLA Ops:
  8.5 7.1 collective-permute-done
  15.6 6.2 broadcast_select_fusion.3
  21.9 9.1 %pad_maximum_fusion.1 = bf16[2,1024,2048]{2,1,0:T(8,128)(2,1)} fusion(bf16[1,1024,2048]{2,1,0:T(8,128)(2,1)} %get-tuple-element.160, bf16[1,1024,2048]{2,1,0:T(8,128)(2,1)S(1)} %get-tuple-element.159), kind=kLoop, calls=%fused_computation.112 | loop fusion | flops 4194304 | bytes 16777216 | tf_op jit(solution)/shard_map/concatenate | solution.py:27
  34.3 261.6 %collective-permute-done.1 = bf16[2,1024,2048]{2,1,0:T(8,128)(2,1)} collective-permute-done((bf16[2,1024,2048]{2,1,0:T(8,128)(2,1)}, bf16[2,1024,2048]{2,1,0:T(8,128)(2,1)}, u32[]{:S(2)}, u32[]{:S(2)}) %collective-permute-start.1) | collective-permute-done | bytes 8388640 | tf_op jit(solution)/shard_map/ppermute | solution.py:25
  295.9 6.3 broadcast_select_fusion.1
  303.9 5.7 copy-done
  309.6 4.3 bitcast_dynamic-update-slice_fusion.1
  313.9 11.9 %fusion.92 = bf16[64,4096]{1,0:T(8,128)(2,1)} fusion(bf16[1,4096,2048]{2,1,0:T(8,128)(2,1)} %all-gather.3.cloned.1.call-done, f32[64,2048]{1,0:T(8,128)S(1)} %get-tuple-element.169), kind=kOutput, calls=%fused_computation.124 | convolution fusion | flops 1074659328 | bytes 17825792 | tf_op jit(solution)/shard_map/dot_general | solution.py:73
  325.9 38.7 %all-reduce.5.cloned.1.call-done = bf16[64,4096]{1,0:T(8,128)(2,1)} async-done(((bf16[64,4096]{1,0:T(8,128)(2,1)}), bf16[64,4096]{1,0:T(8,128)(2,1)}) %all-reduce.5.cloned.1.call-update) | async-done | bytes 524304 | tf_op jit(solution)/shard_map/psum | solution.py:76
  365.8 3.6 collective-permute-start.2
  369.7 9.8 %collective-permute-done.2 = bf16[64,4096]{1,0:T(8,128)(2,1)S(1)} collective-permute-done((bf16[64,4096]{1,0:T(8,128)(2,1)S(1)}, bf16[64,4096]{1,0:T(8,128)(2,1)S(1)}, u32[]{:S(2)}, u32[]{:S(2)}) %collective-permute-start.2) | collective-permute-done | bytes 524320 | tf_op jit(solution)/shard_map/ppermute | solution.py:39
  379.9 9.7 %fusion.187 = (bf16[2,64,2048]{2,1,0:T(8,128)(2,1)S(1)}, f32[64,2048]{1,0:T(8,128)}) fusion(bf16[2,64,2048]{2,1,0:T(8,128)(2,1)S(1)} %get-tuple-element.168, s32[]{:T(128)S(6)} %min.20, pred[]{:T(512)S(6)} %and.72, bf16[4096,2048]{1,0:T(8,128)(2,1)} %bitcast.225, bf16[64,4096]{1,0:T(8,128)(2,1)S(1)} %get-tuple-element.148, f32[4096]{0:T(1024)S(1)} %bitcast.234, ...), kind=kOutput, calls=%fused_computation.235 | convolution fusion | flops 1075576832 | bytes 18366980 | tf_op jit(solution)/shard_map/dot_general | solution.py:71
  389.6 12.1 %fusion.95 = bf16[64,4096]{1,0:T(8,128)(2,1)} fusion(bf16[1,4096,2048]{2,1,0:T(8,128)(2,1)} %all-gather.3.cloned.1.call-done, f32[64,2048]{1,0:T(8,128)} %get-tuple-element.171), kind=kOutput, calls=%fused_computation.125 | convolution fusion | flops 1074659328 | bytes 17825792 | tf_op jit(solution)/shard_map/dot_general | solution.py:73
  404.6 36.6 %all-reduce.7.cloned.1.call-done = bf16[64,4096]{1,0:T(8,128)(2,1)} async-done(((bf16[64,4096]{1,0:T(8,128)(2,1)}), bf16[64,4096]{1,0:T(8,128)(2,1)}) %all-reduce.7.cloned.1.call-update) | async-done | bytes 524304 | tf_op jit(solution)/shard_map/psum | solution.py:76
  442.4 3.7 collective-permute-start.3
  451.0 5.0 collective-permute-done.3
  456.5 9.0 %fusion.186 = (bf16[2,64,2048]{2,1,0:T(8,128)(2,1)S(1)}, f32[64,2048]{1,0:T(8,128)S(1)}) fusion(bf16[2,64,2048]{2,1,0:T(8,128)(2,1)S(1)} %copy-done.7, s32[]{:T(128)S(6)} %min.21, pred[]{:T(512)S(6)} %and.73, bf16[4096,2048]{1,0:T(8,128)(2,1)} %bitcast.226, bf16[64,4096]{1,0:T(8,128)(2,1)S(1)} %get-tuple-element.146, f32[64]{0:T(128)S(1)} %add_rsqrt_fusion, ...), kind=kOutput, calls=%fused_computation.233 | convolution fusion | flops 1075576832 | bytes 18366980 | tf_op jit(solution)/shard_map/dot_general | solution.py:71
  468.2 15.7 %convolution_convert_fusion.4 = bf16[64,4096]{1,0:T(8,128)(2,1)} fusion(bf16[4096,2048]{1,0:T(8,128)(2,1)} %bitcast.227, bf16[1,4096,2048]{2,1,0:T(8,128)(2,1)} %all-gather.3.cloned.1.call-done, f32[2,64,2048]{2,1,0:T(8,128)} %fusion.170, s32[]{:T(128)S(6)} %min.22, bf16[2,64,4096]{2,1,0:T(8,128)(2,1)S(1)} %copy-done.5, pred[]{:T(512)S(6)} %eq.68), kind=kOutput, calls=%fused_computation.123 | convolution fusion | flops 2149187584 | bytes 35127300 | tf_op jit(solution)/shard_map/dot_general | solution.py:84
  486.0 37.3 %all-reduce.9.cloned.1.call-done = bf16[64,4096]{1,0:T(8,128)(2,1)} async-done(((bf16[64,4096]{1,0:T(8,128)(2,1)}), bf16[64,4096]{1,0:T(8,128)(2,1)}) %all-reduce.9.cloned.1.call-update) | async-done | bytes 524304 | tf_op jit(solution)/shard_map/psum | solution.py:87
  528.8 12.2 %collective-permute-done.4 = bf16[64,4096]{1,0:T(8,128)(2,1)} collective-permute-done((bf16[64,4096]{1,0:T(8,128)(2,1)S(1)}, bf16[64,4096]{1,0:T(8,128)(2,1)}, u32[]{:S(2)}, u32[]{:S(2)}) %collective-permute-start.4) | collective-permute-done | bytes 524320 | tf_op jit(solution)/shard_map/ppermute | solution.py:39
  543.3 15.8 %convolution_convert_fusion.3 = bf16[64,4096]{1,0:T(8,128)(2,1)} fusion(bf16[4096,2048]{1,0:T(8,128)(2,1)} %bitcast.228, bf16[64,4096]{1,0:T(8,128)(2,1)S(1)} %get-tuple-element.144, bf16[1,4096,2048]{2,1,0:T(8,128)(2,1)} %all-gather.3.cloned.1.call-done, f32[2,64,2048]{2,1,0:T(8,128)} %fusion.170, s32[]{:T(128)S(6)} %min.23), kind=kOutput, calls=%fused_computation.122 | convolution fusion | flops 2148925440 | bytes 35127300 | tf_op jit(solution)/shard_map/dot_general | solution.py:84
  564.2 4.7 select_bitcast_fusion.1
  568.9 4.8 all-to-all-start
  573.7 22.9 %all-reduce.11.cloned.1.call-done = bf16[64,4096]{1,0:T(8,128)(2,1)} async-done(((bf16[64,4096]{1,0:T(8,128)(2,1)}), bf16[64,4096]{1,0:T(8,128)(2,1)}) %all-reduce.11.cloned.1.call-update) | async-done | bytes 524304 | tf_op jit(solution)/shard_map/psum | solution.py:87
  600.7 13.3 %collective-permute-done.5 = bf16[64,4096]{1,0:T(8,128)(2,1)S(1)} collective-permute-done((bf16[64,4096]{1,0:T(8,128)(2,1)S(1)}, bf16[64,4096]{1,0:T(8,128)(2,1)S(1)}, u32[]{:S(2)}, u32[]{:S(2)}) %collective-permute-start.5) | collective-permute-done | bytes 524320 | tf_op jit(solution)/shard_map/ppermute | solution.py:39
  620.8 4.7 select_bitcast_fusion
  625.5 5.0 all-to-all-start.1
  630.6 6.4 copy.34
  637.0 41.7 %all-to-all-done.1 = bf16[128,32,512]{2,0,1:T(8,128)(2,1)} async-done(((bf16[128,32,512]{2,0,1:T(8,128)(2,1)}), bf16[128,32,512]{2,0,1:T(8,128)(2,1)}, u32[]{:S(2)}, u32[]{:S(2)}) %all-to-all-start.1) | async-done | bytes 4194336 | tf_op jit(solution)/shard_map/all_to_all | solution.py:175
  678.7 10.9 %convolution_convert_fusion.2 = bf16[4,8,512,512]{3,2,1,0:T(8,128)(2,1)} fusion(bf16[4,128,8,512]{1,3,2,0:T(8,128)(2,1)} %bitcast.231, bf16[4,128,8,512]{3,1,2,0:T(8,128)(2,1)} %bitcast.37), kind=kOutput, calls=%fused_computation.111 | convolution fusion | flops 2155872256 | bytes 25165824 | tf_op jit(solution)/shard_map/snbk,snbl->sbkl/dot_general | solution.py:179
  689.6 9.6 %convert_reduce_fusion = f32[8,512,512]{2,1,0:T(8,128)S(1)} fusion(bf16[4,8,512,512]{3,2,1,0:T(8,128)(2,1)} %convolution_convert_fusion.2), kind=kLoop, calls=%fused_computation.101 | loop fusion | flops 14680064 | bytes 25165824 | tf_op jit(solution)/shard_map/reduce_sum | solution.py:181
  699.2 19.7 %bitcast_add_fusion = f32[8,512,512]{2,1,0:T(8,128)} fusion(f32[1,8,512,512]{3,2,1,0:T(8,128)} %param.22, f32[8,512,512]{2,1,0:T(8,128)S(1)} %convert_reduce_fusion), kind=kOutput, calls=%fused_computation.113 | convolution fusion | flops 12893290496 | bytes 25165824 | tf_op jit(solution)/shard_map/sji,sjk->sik/dot_general | solution.py:189
  718.9 17.6 %bitcast_add_fusion.1 = f32[8,512,512]{2,1,0:T(8,128)} fusion(f32[1,8,512,512]{3,2,1,0:T(8,128)} %param.21, f32[8,512,512]{2,1,0:T(8,128)S(1)} %convert_reduce_fusion), kind=kOutput, calls=%fused_computation.114 | convolution fusion | flops 12893290496 | bytes 25165824 | tf_op jit(solution)/shard_map/sij,skj->sik/dot_general | solution.py:185
  736.5 118.7 %while.12 = (s32[]{:T(128)}, bf16[8,512,512]{2,1,0:T(8,128)(2,1)}, bf16[8,512,512]{2,1,0:T(8,128)(2,1)}, pred[8]{0:T(512)(128)(4,1)S(1)}, bf16[8,512,512]{2,1,0:...) while((s32[]{:T(128)}, bf16[8,512,512]{2,1,0:T(8,128)(2,1)}, ...), condition=%wide.region_18.19_spmd, body=%wide.region_13.18_spmd.sunk | while | flops 16121331712 | bytes 28315412 | solution.py:210
  748.7 31.2 %conditional.2 = (bf16[1,512,512]{2,1,0:T(8,128)(2,1)S(1)}, bf16[1,512,512]{2,1,0:T(8,128)(2,1)S(1)}) conditional(s32[]{:T(128)} %bitcast.220, (bf16[8,512,512]{2,1,0:T(8,128)(2,1)}, s32[]{:T(128)}, bf16[8,512,512]{2,1,0:T(8,128)(2,1)}) %tuple.67, (f32[8,512,512]{2,1,0:T(8,128)}, s32[]{:T(128)}, f32[8,512,512]{2,1,0:T(8,128)}) %tuple.68), branch_computations={%region_14.14_spmd, %region_15.17_spmd} | conditional | flops 16121331712 | bytes 26217596 | solution.py:200
  751.9 3.6 fusion.6
  760.5 3.1 fusion.15
  766.2 3.7 fusion.3
  771.7 3.1 select_subtract_fusion.2
  782.2 31.1 %conditional.2 = (bf16[1,512,512]{2,1,0:T(8,128)(2,1)S(1)}, bf16[1,512,512]{2,1,0:T(8,128)(2,1)S(1)}) conditional(s32[]{:T(128)} %bitcast.220, (bf16[8,512,512]{2,1,0:T(8,128)(2,1)}, s32[]{:T(128)}, bf16[8,512,512]{2,1,0:T(8,128)(2,1)}) %tuple.67, (f32[8,512,512]{2,1,0:T(8,128)}, s32[]{:T(128)}, f32[8,512,512]{2,1,0:T(8,128)}) %tuple.68), branch_computations={%region_14.14_spmd, %region_15.17_spmd} | conditional | flops 16121331712 | bytes 26217596 | solution.py:200
  785.4 3.6 fusion.6
  790.9 3.1 select_subtract_fusion
  799.7 3.6 fusion.3
  815.6 31.1 %conditional.2 = (bf16[1,512,512]{2,1,0:T(8,128)(2,1)S(1)}, bf16[1,512,512]{2,1,0:T(8,128)(2,1)S(1)}) conditional(s32[]{:T(128)} %bitcast.220, (bf16[8,512,512]{2,1,0:T(8,128)(2,1)}, s32[]{:T(128)}, bf16[8,512,512]{2,1,0:T(8,128)(2,1)}) %tuple.67, (f32[8,512,512]{2,1,0:T(8,128)}, s32[]{:T(128)}, f32[8,512,512]{2,1,0:T(8,128)}) %tuple.68), branch_computations={%region_14.14_spmd, %region_15.17_spmd} | conditional | flops 16121331712 | bytes 26217596 | solution.py:200
  818.8 3.6 fusion.6
  833.1 3.6 fusion.3
  841.7 3.1 fusion.14
  855.2 12.3 %convert_bitcast_fusion = bf16[1,8,512,512]{3,2,1,0:T(8,128)(2,1)} fusion(bf16[8,512,512]{2,1,0:T(8,128)(2,1)} %get-tuple-element.120, bf16[8,512,512]{2,1,0:T(8,128)(2,1)} %get-tuple-element.121, f32[8,512,512]{2,1,0:T(8,128)} %copy-done.1), kind=kOutput, calls=%fused_computation.129 | convolution fusion | flops 4303355904 | bytes 20971520 | tf_op jit(solution)/shard_map/sij,sjk->sik/dot_general | solution.py:217
  (143 shorter events, 125.9 us)
Async XLA Ops:
  7.2 306.7 %all-gather.3.cloned.1.call-start = ((), (), s32[]{:S(2)}) async-start(), calls=%async_computation.6 | async-start | bytes 20971520 | tf_op jit(solution)/shard_map/all_gather | solution.py:122
  7.9 356.7 %all-reduce.5.cloned.1.call-start = ((), (), s32[]{:S(2)}) async-start(), calls=%async_computation.2 | async-start | bytes 1048576 | tf_op jit(solution)/shard_map/psum | solution.py:76
  7.9 7.7 collective-permute-start
  21.9 9.1 %copy-start.2 = (bf16[1,1024,2048]{2,1,0:T(8,128)(2,1)}, bf16[1,1024,2048]{2,1,0:T(8,128)(2,1)S(1)}, u32[]{:S(2)}) copy-start(bf16[1,1024,2048]{2,1,0:T(8,128)(2,1)S(1)} %get-tuple-element.159) | copy-start | bytes 12582916
  21.9 12.2 %copy-start.3 = (bf16[2,64,4096]{2,1,0:T(8,128)(2,1)S(1)}, bf16[2,64,4096]{2,1,0:T(8,128)(2,1)}, u32[]{:S(2)}) copy-start(bf16[2,64,4096]{2,1,0:T(8,128)(2,1)} %param.16) | copy-start | bytes 3145732
  31.0 264.9 %collective-permute-start.1 = (bf16[2,1024,2048]{2,1,0:T(8,128)(2,1)}, bf16[2,1024,2048]{2,1,0:T(8,128)(2,1)}, u32[]{:S(2)}, u32[]{:S(2)}) collective-permute-start(bf16[2,1024,2048]{2,1,0:T(8,128)(2,1)} %pad_maximum_fusion.1), channel_id=1, source_target_pairs={{0,8},{4,12},{8,0},{12,4},{1,9},{5,13},{9,1},{13,5},{2,10},{6,14},... | collective-permute-start | bytes 25165832 | tf_op jit(solution)/shard_map/ppermute | solution.py:25
  302.2 7.3 copy-start.11
  303.8 5.7 copy-start
  313.8 12.0 %copy-start.10 = (f32[64,2048]{1,0:T(8,128)}, f32[64,2048]{1,0:T(8,128)S(1)}, u32[]{:S(2)}) copy-start(f32[64,2048]{1,0:T(8,128)S(1)} %get-tuple-element.169) | copy-start | bytes 1572868
  313.9 50.8 %copy-start.4 = (bf16[2,64,4096]{2,1,0:T(8,128)(2,1)S(1)}, bf16[2,64,4096]{2,1,0:T(8,128)(2,1)}, u32[]{:S(2)}) copy-start(bf16[2,64,4096]{2,1,0:T(8,128)(2,1)} %param.16) | copy-start | bytes 3145732
  325.8 115.3 %all-reduce.7.cloned.1.call-start = ((), (), s32[]{:S(2)}) async-start(), calls=%async_computation.3 | async-start | bytes 1048576 | tf_op jit(solution)/shard_map/psum | solution.py:76
  365.8 13.6 %collective-permute-start.2 = (bf16[64,4096]{1,0:T(8,128)(2,1)S(1)}, bf16[64,4096]{1,0:T(8,128)(2,1)S(1)}, u32[]{:S(2)}, u32[]{:S(2)}) collective-permute-start(bf16[64,4096]{1,0:T(8,128)(2,1)S(1)} %fusion.129), channel_id=1, source_target_pairs={{0,16},{1,17},{2,18},{3,19},{4,20},{5,21},{6,22},{7,23},{8,24},{9,... | collective-permute-start | bytes 1572872 | tf_op jit(solution)/shard_map/ppermute | solution.py:39
  389.6 13.2 %copy-start.6 = (bf16[2,64,2048]{2,1,0:T(8,128)(2,1)}, bf16[2,64,2048]{2,1,0:T(8,128)(2,1)S(1)}, u32[]{:S(2)}) copy-start(bf16[2,64,2048]{2,1,0:T(8,128)(2,1)S(1)} %get-tuple-element.170) | copy-start | bytes 1572868
  389.6 12.9 %copy-start.12 = (s32[2,16,8]{1,2,0:T(8,128)S(1)}, s32[2,16,8]{1,2,0:T(8,128)}, u32[]{:S(2)}) copy-start(s32[2,16,8]{1,2,0:T(8,128)} %param.26) | copy-start | bytes 3076
  389.6 12.9 %copy-start.13 = (s32[2,16,8]{1,2,0:T(8,128)S(1)}, s32[2,16,8]{1,2,0:T(8,128)}, u32[]{:S(2)}) copy-start(s32[2,16,8]{1,2,0:T(8,128)} %param.25) | copy-start | bytes 3076
  401.8 121.5 %all-reduce.9.cloned.1.call-start = ((), (), s32[]{:S(2)}) async-start(), calls=%async_computation.4 | async-start | bytes 1048576 | tf_op jit(solution)/shard_map/psum | solution.py:87
  441.1 15.3 %copy-start.7 = (bf16[2,64,2048]{2,1,0:T(8,128)(2,1)S(1)}, bf16[2,64,2048]{2,1,0:T(8,128)(2,1)}, u32[]{:S(2)}) copy-start(bf16[2,64,2048]{2,1,0:T(8,128)(2,1)} %copy-done.6) | copy-start | bytes 1572868
  442.4 13.6 %collective-permute-start.3 = (bf16[64,4096]{1,0:T(8,128)(2,1)S(1)}, bf16[64,4096]{1,0:T(8,128)(2,1)S(1)}, u32[]{:S(2)}, u32[]{:S(2)}) collective-permute-start(bf16[64,4096]{1,0:T(8,128)(2,1)S(1)} %fusion.138), channel_id=1, source_target_pairs={{0,16},{1,17},{2,18},{3,19},{4,20},{5,21},{6,22},{7,23},{8,24},{9,... | collective-permute-start | bytes 1572872 | tf_op jit(solution)/shard_map/ppermute | solution.py:39
  456.5 11.8 %copy-start.5 = (bf16[2,64,4096]{2,1,0:T(8,128)(2,1)S(1)}, bf16[2,64,4096]{2,1,0:T(8,128)(2,1)}, u32[]{:S(2)}) copy-start(bf16[2,64,4096]{2,1,0:T(8,128)(2,1)} %param.17) | copy-start | bytes 3145732
  465.5 0.8 copy-start.8
  484.0 112.7 %all-reduce.11.cloned.1.call-start = ((), (), s32[]{:S(2)}) async-start(), calls=%async_computation.5 | async-start | bytes 1048576 | tf_op jit(solution)/shard_map/psum | solution.py:87
  526.3 14.7 %collective-permute-start.4 = (bf16[64,4096]{1,0:T(8,128)(2,1)S(1)}, bf16[64,4096]{1,0:T(8,128)(2,1)}, u32[]{:S(2)}, u32[]{:S(2)}) collective-permute-start(bf16[64,4096]{1,0:T(8,128)(2,1)S(1)} %fusion.140), channel_id=1, source_target_pairs={{16,0},{17,1},{18,2},{19,3},{20,4},{21,5},{22,6},{23,7},{24,8},{25... | collective-permute-start | bytes 1572872 | tf_op jit(solution)/shard_map/ppermute | solution.py:39
  543.3 15.8 %copy-start.9 = (bf16[2,64,2048]{2,1,0:T(8,128)(2,1)S(1)}, bf16[2,64,2048]{2,1,0:T(8,128)(2,1)}, u32[]{:S(2)}) copy-start(bf16[2,64,2048]{2,1,0:T(8,128)(2,1)} %copy-done.8) | copy-start | bytes 1572868
  568.9 56.6 %all-to-all-start = ((bf16[128,32,512]{2,0,1:T(8,128)(2,1)}), bf16[128,32,512]{2,0,1:T(8,128)(2,1)}, u32[]{:S(2)}, u32[]{:S(2)}) async-start(bf16[128,32,512]{2,0,1:T(8,128)(2,1)} %select_bitcast_fusion.1), calls=%async_computation | async-start | bytes 8388608 | tf_op jit(solution)/shard_map/all_to_all | solution.py:174
  599.4 14.6 %collective-permute-start.5 = (bf16[64,4096]{1,0:T(8,128)(2,1)S(1)}, bf16[64,4096]{1,0:T(8,128)(2,1)S(1)}, u32[]{:S(2)}, u32[]{:S(2)}) collective-permute-start(bf16[64,4096]{1,0:T(8,128)(2,1)S(1)} %fusion.142), channel_id=1, source_target_pairs={{16,0},{17,1},{18,2},{19,3},{20,4},{21,5},{22,6},{23,7},{24,8},{25... | collective-permute-start | bytes 1572872 | tf_op jit(solution)/shard_map/ppermute | solution.py:39
  625.5 53.2 %all-to-all-start.1 = ((bf16[128,32,512]{2,0,1:T(8,128)(2,1)}), bf16[128,32,512]{2,0,1:T(8,128)(2,1)}, u32[]{:S(2)}, u32[]{:S(2)}) async-start(bf16[128,32,512]{2,0,1:T(8,128)(2,1)} %select_bitcast_fusion), calls=%async_computation.1 | async-start | bytes 8388608 | tf_op jit(solution)/shard_map/all_to_all | solution.py:175
  699.2 19.7 %copy-start.1 = (f32[8,512,512]{2,1,0:T(8,128)}, f32[8,512,512]{2,1,0:T(8,128)S(1)}, u32[]{:S(2)}) copy-start(f32[8,512,512]{2,1,0:T(8,128)S(1)} %convert_reduce_fusion) | copy-start | bytes 25165828
Sparse Core Ops, SparseCore 0:
  9.5 189.4 all-gather.2
  326.0 38.6 all-reduce.4
  401.9 39.1 all-reduce.6
  484.1 39.1 all-reduce.8
  559.2 37.4 all-reduce.10
